TPU v7x, 32 devices: a whole 2x2x4 slice. The times are simulated.
32 devices in a mesh: groups: 2 (over x), blk: 16 (over z, y, core).
Axes of the slice: x: 2, y: 2, z: 4, core: 2. Of those that a mesh axis runs over, the one named last changes fastest.
Arguments:
- queries: bfloat16 [24576, 1536], P(('groups', 'blk')), parts along dimension 0, may hold values from -20 to 20
- keys: bfloat16 [24576, 1536], P(('groups', 'blk')), parts along dimension 0, may hold values from -6 to 6
- values: bfloat16 [24576, 1536], P(('groups', 'blk')), parts along dimension 0, may hold values from -6 to 6
- neighbours: int32 [64, 7], P(('groups', 'blk')), parts along dimension 0, may hold values from -1 to 31, as said below
Outputs:
- attended: bfloat16 [24576, 1536], P(('groups', 'blk')), parts along dimension 0
There are 2 independent parts, one for each index of `groups`. A program takes and returns all parts, laid end to end along the dimension named above; each array names one. Nothing has to cross between parts.
Inputs may be any that keep to these rules, and one draw needn't show every extreme that they name: `neighbours`: entry 0 of row t is t itself. Every other non-negative entry names a distinct tile of a frame block at most two blocks away from tile t's block; a slot is -1 only where its drawn tile falls outside the clip.
All inputs are finite; a program needn't handle non-finite values.
Results may differ from a plain program's by a relative error of at most 0.0048.
Values may be sent and summed in bfloat16 or wider, within the bound.
A program may use at most 128 MiB of HBM per device.

v0:
```python
import jax
import jax.numpy as jnp
from jax import lax
from jax.sharding import PartitionSpec as P

HD = 128


def passed_along(value, axis, steps):
    count = lax.axis_size(axis)
    initial, last = (max(0, -steps), min(count, count - steps))
    return lax.ppermute(value, axis, [(source, source + steps) for source in range(initial, last)])


def on_device(queries, keys, values, neighbours):
    tokens_here = queries.shape[0]
    tiles_here = neighbours.shape[0]
    slots = neighbours.shape[1]
    tile_len = tokens_here // tiles_here
    width = queries.shape[1]
    head_size = HD
    head_count = width // head_size
    scale = head_size ** (-0.5)
    block = lax.axis_index("blk")
    near_low = passed_along((keys, values), "blk", 1)
    near_high = passed_along((keys, values), "blk", -1)
    far_low = passed_along((keys, values), "blk", 2)
    far_high = passed_along((keys, values), "blk", -2)
    window_keys = jnp.concatenate(
        [far_low[0], near_low[0], keys, near_high[0], far_high[0]], axis=0
    )
    window_values = jnp.concatenate(
        [far_low[1], near_low[1], values, near_high[1], far_high[1]], axis=0
    )
    window_keys = window_keys.reshape(5 * tiles_here, tile_len, width)
    window_values = window_values.reshape(5 * tiles_here, tile_len, width)
    base = (block - 2) * tiles_here
    query_tiles = queries.reshape(tiles_here, tile_len, width)

    def one_tile(tile_here):
        named = neighbours[tile_here]
        valid = named >= 0
        local = jnp.where(valid, named - base, 0)
        key_rows = window_keys[local].reshape(slots * tile_len, width)
        value_rows = window_values[local].reshape(slots * tile_len, width)
        query_rows = query_tiles[tile_here]
        key_mask = jnp.repeat(valid, tile_len)[None, :]

        def one_head(head, output):
            start = head * head_size
            query_cols = lax.dynamic_slice_in_dim(query_rows, start, head_size, 1)
            key_cols = lax.dynamic_slice_in_dim(key_rows, start, head_size, 1)
            value_cols = lax.dynamic_slice_in_dim(value_rows, start, head_size, 1)
            scores = (
                lax.dot_general(
                    query_cols,
                    key_cols,
                    (((1,), (1,)), ((), ())),
                    preferred_element_type=jnp.float32,
                )
                * scale
            )
            scores = jnp.where(key_mask, scores, -jnp.inf)
            peak = jnp.max(scores, axis=1, keepdims=True)
            weights = jnp.exp(scores - peak)
            total = jnp.sum(weights, axis=1, keepdims=True)
            rounded = weights.astype(jnp.bfloat16)
            summed = jnp.dot(rounded, value_cols, preferred_element_type=jnp.float32)
            result = (summed / total).astype(jnp.bfloat16)
            return lax.dynamic_update_slice_in_dim(output, result, start, 1)

        empty = jnp.zeros((tile_len, width), jnp.bfloat16)
        return lax.fori_loop(0, head_count, one_head, empty)

    output = lax.map(one_tile, jnp.arange(tiles_here, dtype=jnp.int32))
    return output.reshape(tokens_here, width)


def solution(mesh):
    in_specs = (
        P(("groups", "blk"), None),
        P(("groups", "blk"), None),
        P(("groups", "blk"), None),
        P(("groups", "blk"), None),
    )
    out_specs = P(("groups", "blk"), None)
    return jax.shard_map(
        on_device, mesh=mesh, in_specs=in_specs, out_specs=out_specs, check_vma=False
    )
```

profile of v0, /device:TPU:1, one launch (start us, length us, event | category | flops | bytes accessed | tf_op | source)
XLA Modules:
  0.0 480.4 jit_solution(3247733563765416501)
XLA Ops:
  0.0 5.5 %collective-permute-start.4 = (bf16[768,1536]{1,0:T(8,128)(2,1)}, bf16[768,1536]{1,0:T(8,128)(2,1)}, u32[]{:S(2)}, u32[]{:S(2)}) collective-permute-start(bf16[768,1536]{1,0:T(8,128)(2,1)} %param.10), channel_id=1, source_target_pairs={{0,2},{1,3},{2,4},{3,5},{4,6},{5,7},{6,8},{7,9},{8,10},{9,11},{10,... | collective-permute-start | bytes 7077896 | tf_op jit(solution)/shard_map/ppermute | solution.py:12
  5.5 2.6 collective-permute-start.5
  8.1 4.6 collective-permute-start
  12.7 1.9 collective-permute-start.1
  14.6 3.8 collective-permute-start.6
  18.4 61.2 %collective-permute-done.4 = bf16[768,1536]{1,0:T(8,128)(2,1)} collective-permute-done((bf16[768,1536]{1,0:T(8,128)(2,1)}, bf16[768,1536]{1,0:T(8,128)(2,1)}, u32[]{:S(2)}, u32[]{:S(2)}) %collective-permute-start.4) | collective-permute-done | bytes 2359328 | tf_op jit(solution)/shard_map/ppermute | solution.py:12
  80.9 125.1 %collective-permute-done.5 = bf16[768,1536]{1,0:T(8,128)(2,1)} collective-permute-done((bf16[768,1536]{1,0:T(8,128)(2,1)}, bf16[768,1536]{1,0:T(8,128)(2,1)}, u32[]{:S(2)}, u32[]{:S(2)}) %collective-permute-start.5) | collective-permute-done | bytes 2359328 | tf_op jit(solution)/shard_map/ppermute | solution.py:12
  206.0 1.9 collective-permute-start.2
  209.7 48.0 %collective-permute-done = bf16[768,1536]{1,0:T(8,128)(2,1)} collective-permute-done((bf16[768,1536]{1,0:T(8,128)(2,1)}, bf16[768,1536]{1,0:T(8,128)(2,1)}, u32[]{:S(2)}, u32[]{:S(2)}) %collective-permute-start) | collective-permute-done | bytes 2359328 | tf_op jit(solution)/shard_map/ppermute | solution.py:12
  262.8 45.5 %collective-permute-done.1 = bf16[768,1536]{1,0:T(8,128)(2,1)} collective-permute-done((bf16[768,1536]{1,0:T(8,128)(2,1)}, bf16[768,1536]{1,0:T(8,128)(2,1)}, u32[]{:S(2)}, u32[]{:S(2)}) %collective-permute-start.1) | collective-permute-done | bytes 2359328 | tf_op jit(solution)/shard_map/ppermute | solution.py:12
  314.3 3.9 copy-done
  318.2 3.6 copy-done.1
  321.8 158.6 %while.25 = (s32[]{:T(128)}, bf16[2,384,1536]{2,1,0:T(8,128)(2,1)}, s32[2]{0:T(128)S(1)}, bf16[2,384,1536]{2,1,0:T(8,128)(2,1)}, s32[2,7]{1,0:T(2,128)S(1)}, /*i...) while((s32[]{:T(128)}, bf16[2,384,1536]{2,1,0:T(8,128)(2,1)}, ...), condition=%wide.region_5.6_spmd, body=%wide.region_0.5_spmd.sunk | while | flops 535806272 | bytes 52914680 | solution.py:75
  324.4 9.2 %gather_fusion = bf16[7,384,1536]{2,1,0:T(8,128)(2,1)} fusion(bf16[10,384,1536]{2,1,0:T(8,128)(2,1)} %get-tuple-element.375, s32[1024]{0:T(1024)S(1)} %pad_clamp_fusion.2), kind=kCustom, calls=%fused_computation.clone.1 | custom fusion | bytes 16515100 | tf_op jit(solution)/shard_map/while/body/eval_jaxpr/gather | solution.py:44
  333.6 9.2 %gather_fusion.1 = bf16[7,384,1536]{2,1,0:T(8,128)(2,1)} fusion(bf16[10,384,1536]{2,1,0:T(8,128)(2,1)} %get-tuple-element.376, s32[1024]{0:T(1024)S(1)} %pad_clamp_fusion.2), kind=kCustom, calls=%fused_computation.1.clone.1 | custom fusion | bytes 16515100 | tf_op jit(solution)/shard_map/while/body/eval_jaxpr/gather | solution.py:45
  344.2 55.8 %while.26 = (s32[]{:T(128)}, bf16[384,1536]{1,0:T(8,128)(2,1)S(1)}, bf16[384,1536]{1,0:T(8,128)(2,1)S(1)}, bf16[2688,1536]{1,0:T(8,128)(2,1)}, bf16[2688,1536]{1...) while((s32[]{:T(128)}, bf16[384,1536]{1,0:T(8,128)(2,1)S(1)}, ...), condition=%wide.region_4.4_spmd.clone, body=%wide.region_1.3_spmd.clone.sunk | while | flops 535805184 | bytes 13981210 | solution.py:73
  344.3 1.9 fusion.34
  346.9 1.9 fusion.36
  348.9 1.9 fusion.34
  351.6 1.9 fusion.36
  353.6 1.9 fusion.34
  356.2 1.9 fusion.36
  358.2 1.9 fusion.34
  360.9 1.9 fusion.36
  362.9 1.9 fusion.34
  365.5 1.9 fusion.36
  367.5 1.9 fusion.34
  370.2 1.9 fusion.36
  372.2 1.9 fusion.34
  374.8 1.9 fusion.36
  376.8 1.9 fusion.34
  379.5 1.9 fusion.36
  381.5 1.9 fusion.34
  384.1 1.9 fusion.36
  386.1 1.9 fusion.34
  388.8 1.9 fusion.36
  390.8 1.9 fusion.34
  393.4 1.9 fusion.36
  395.4 1.9 fusion.34
  398.1 1.9 fusion.36
  403.6 9.2 %gather_fusion = bf16[7,384,1536]{2,1,0:T(8,128)(2,1)} fusion(bf16[10,384,1536]{2,1,0:T(8,128)(2,1)} %get-tuple-element.375, s32[1024]{0:T(1024)S(1)} %pad_clamp_fusion.2), kind=kCustom, calls=%fused_computation.clone.1 | custom fusion | bytes 16515100 | tf_op jit(solution)/shard_map/while/body/eval_jaxpr/gather | solution.py:44
  412.8 9.2 %gather_fusion.1 = bf16[7,384,1536]{2,1,0:T(8,128)(2,1)} fusion(bf16[10,384,1536]{2,1,0:T(8,128)(2,1)} %get-tuple-element.376, s32[1024]{0:T(1024)S(1)} %pad_clamp_fusion.2), kind=kCustom, calls=%fused_computation.1.clone.1 | custom fusion | bytes 16515100 | tf_op jit(solution)/shard_map/while/body/eval_jaxpr/gather | solution.py:45
  423.4 55.8 %while.26 = (s32[]{:T(128)}, bf16[384,1536]{1,0:T(8,128)(2,1)S(1)}, bf16[384,1536]{1,0:T(8,128)(2,1)S(1)}, bf16[2688,1536]{1,0:T(8,128)(2,1)}, bf16[2688,1536]{1...) while((s32[]{:T(128)}, bf16[384,1536]{1,0:T(8,128)(2,1)S(1)}, ...), condition=%wide.region_4.4_spmd.clone, body=%wide.region_1.3_spmd.clone.sunk | while | flops 535805184 | bytes 13981210 | solution.py:73
  423.5 1.9 fusion.34
  426.2 1.9 fusion.36
  428.2 1.9 fusion.34
  430.8 1.9 fusion.36
  432.8 1.9 fusion.34
  435.5 1.9 fusion.36
  437.5 1.9 fusion.34
  440.2 1.9 fusion.36
  442.2 1.9 fusion.34
  444.8 1.9 fusion.36
  446.8 1.9 fusion.34
  451.5 1.9 fusion.34
  454.1 1.9 fusion.36
  456.1 1.9 fusion.34
  458.8 1.9 fusion.36
  460.8 1.9 fusion.34
  465.4 1.9 fusion.34
  470.1 1.9 fusion.34
  472.7 1.9 fusion.36
  474.7 1.9 fusion.34
  477.4 1.9 fusion.36
  (115 shorter events, 45.2 us)
Async XLA Ops:
  0.0 257.7 %copy-start.3 = (bf16[768,1536]{1,0:T(8,128)(2,1)S(1)}, bf16[768,1536]{1,0:T(8,128)(2,1)}, u32[]{:S(2)}) copy-start(bf16[768,1536]{1,0:T(8,128)(2,1)} %param.9) | copy-start | bytes 7077892
  0.0 79.6 %collective-permute-start.4 = (bf16[768,1536]{1,0:T(8,128)(2,1)}, bf16[768,1536]{1,0:T(8,128)(2,1)}, u32[]{:S(2)}, u32[]{:S(2)}) collective-permute-start(bf16[768,1536]{1,0:T(8,128)(2,1)} %param.10), channel_id=1, source_target_pairs={{0,2},{1,3},{2,4},{3,5},{4,6},{5,7},{6,8},{7,9},{8,10},{9,11},{10,... | collective-permute-start | bytes 7077896 | tf_op jit(solution)/shard_map/ppermute | solution.py:12
  5.5 200.5 %collective-permute-start.5 = (bf16[768,1536]{1,0:T(8,128)(2,1)}, bf16[768,1536]{1,0:T(8,128)(2,1)}, u32[]{:S(2)}, u32[]{:S(2)}) collective-permute-start(bf16[768,1536]{1,0:T(8,128)(2,1)} %param.10), channel_id=1, source_target_pairs={{0,1},{1,2},{2,3},{3,4},{4,5},{5,6},{6,7},{7,8},{8,9},{9,10},{10,1... | collective-permute-start | bytes 7077896 | tf_op jit(solution)/shard_map/ppermute | solution.py:12
  8.1 249.6 %collective-permute-start = (bf16[768,1536]{1,0:T(8,128)(2,1)}, bf16[768,1536]{1,0:T(8,128)(2,1)}, u32[]{:S(2)}, u32[]{:S(2)}) collective-permute-start(bf16[768,1536]{1,0:T(8,128)(2,1)} %param.9), channel_id=1, source_target_pairs={{0,2},{1,3},{2,4},{3,5},{4,6},{5,7},{6,8},{7,9},{8,10},{9,11},{10,... | collective-permute-start | bytes 7077896 | tf_op jit(solution)/shard_map/ppermute | solution.py:12
  12.7 295.6 %collective-permute-start.1 = (bf16[768,1536]{1,0:T(8,128)(2,1)}, bf16[768,1536]{1,0:T(8,128)(2,1)}, u32[]{:S(2)}, u32[]{:S(2)}) collective-permute-start(bf16[768,1536]{1,0:T(8,128)(2,1)} %param.9), channel_id=1, source_target_pairs={{0,1},{1,2},{2,3},{3,4},{4,5},{5,6},{6,7},{7,8},{8,9},{9,10},{10,1... | collective-permute-start | bytes 7077896 | tf_op jit(solution)/shard_map/ppermute | solution.py:12
  14.6 295.7 %collective-permute-start.6 = (bf16[768,1536]{1,0:T(8,128)(2,1)}, bf16[768,1536]{1,0:T(8,128)(2,1)}, u32[]{:S(2)}, u32[]{:S(2)}) collective-permute-start(bf16[768,1536]{1,0:T(8,128)(2,1)} %param.10), channel_id=1, source_target_pairs={{1,0},{2,1},{3,2},{4,3},{5,4},{6,5},{7,6},{8,7},{9,8},{10,9},{11,1... | collective-permute-start | bytes 7077896 | tf_op jit(solution)/shard_map/ppermute | solution.py:12
  79.6 232.5 %collective-permute-start.7 = (bf16[768,1536]{1,0:T(8,128)(2,1)}, bf16[768,1536]{1,0:T(8,128)(2,1)}, u32[]{:S(2)}, u32[]{:S(2)}) collective-permute-start(bf16[768,1536]{1,0:T(8,128)(2,1)} %param.10), channel_id=1, source_target_pairs={{2,0},{3,1},{4,2},{5,3},{6,4},{7,5},{8,6},{9,7},{10,8},{11,9},{12,... | collective-permute-start | bytes 7077896 | tf_op jit(solution)/shard_map/ppermute | solution.py:12
  80.9 179.9 %copy-start.2 = (bf16[768,1536]{1,0:T(8,128)(2,1)S(1)}, bf16[768,1536]{1,0:T(8,128)(2,1)}, u32[]{:S(2)}) copy-start(bf16[768,1536]{1,0:T(8,128)(2,1)} %param.10) | copy-start | bytes 7077892
  206.0 107.9 %collective-permute-start.2 = (bf16[768,1536]{1,0:T(8,128)(2,1)}, bf16[768,1536]{1,0:T(8,128)(2,1)S(1)}, u32[]{:S(2)}, u32[]{:S(2)}) collective-permute-start(bf16[768,1536]{1,0:T(8,128)(2,1)} %param.9), channel_id=1, source_target_pairs={{1,0},{2,1},{3,2},{4,3},{5,4},{6,5},{7,6},{8,7},{9,8},{10,9},{11,1... | collective-permute-start | bytes 7077896 | tf_op jit(solution)/shard_map/ppermute | solution.py:12
  257.7 56.4 %collective-permute-start.3 = (bf16[768,1536]{1,0:T(8,128)(2,1)S(1)}, bf16[768,1536]{1,0:T(8,128)(2,1)S(1)}, u32[]{:S(2)}, u32[]{:S(2)}) collective-permute-start(bf16[768,1536]{1,0:T(8,128)(2,1)S(1)} %copy-done.3), channel_id=1, source_target_pairs={{2,0},{3,1},{4,2},{5,3},{6,4},{7,5},{8,6},{9,7},{10,8},{11,9},{12,... | collective-permute-start | bytes 7077896 | tf_op jit(solution)/shard_map/ppermute | solution.py:12
  313.9 4.3 copy-start
  313.9 7.9 %copy-start.4 = (s32[2,7]{1,0:T(2,128)S(1)}, s32[2,7]{1,0:T(2,128)}, u32[]{:S(2)}) copy-start(s32[2,7]{1,0:T(2,128)} %param.11) | copy-start | bytes 172
  314.3 7.5 %copy-start.1 = (bf16[3840,1536]{1,0:T(8,128)(2,1)}, bf16[3840,1536]{1,0:T(8,128)(2,1)S(1)}, u32[]{:S(2)}) copy-start(bf16[3840,1536]{1,0:T(8,128)(2,1)S(1)} %constant_dynamic-update-slice_fusion) | copy-start | bytes 35389444
where the time goes:
time: 483 us; the launch traced here: 480 us
  waiting for transfers between devices  280 us (58%)
  matrix products  91.9 us (19%)
  local copies, waits for them, and re-layouts  64.2 us (13%)
  starting transfers between devices  22.8 us (5%)
  other arithmetic  16.9 us (3%)
    ppermute x8, waiting for transfers between devices, passed_along(): lax.ppermute(value, axis, [(source, source + steps) for source in range(i...  280 us
    dot_general x24, matrix products, one_head(): lax.dot_general(query_cols, key_cols, (((1,), (1,)), ((), ())), preferred...  46.6 us
    dot_general x24, matrix products, one_head(): summed = jnp.dot(rounded, value_cols, preferred_element_type=jnp.float32)  45.3 us
    ppermute x8, starting transfers between devices, passed_along(): lax.ppermute(value, axis, [(source, source + steps) for source in range(i...  22.8 us
    gather x2, local copies, waits for them, and re-layouts, one_tile(): key_rows = window_keys[local].reshape(slots * tile_len, width)  18.4 us
    gather x2, local copies, waits for them, and re-layouts, one_tile(): value_rows = window_values[local].reshape(slots * tile_len, width)  18.3 us
    unnamed x18, local copies, waits for them, and re-layouts  17.1 us
    reduce_sum x24, other arithmetic, one_head(): total = jnp.sum(weights, axis=1, keepdims=True)  16.9 us
  transfers between devices with their start and end apart: 8, of which 4 were waited for; matrix products, arithmetic and copies ran while one was open for 2% of the time, Pallas kernels for 0%

commit v1 on v0

v1 whole, which is shorter than its diff:
```python
import functools
import math

import jax
import jax.numpy as jnp
from jax import lax
from jax.experimental import pallas as pl
from jax.experimental.pallas import tpu as pltpu
from jax.sharding import PartitionSpec as P

HD = 128
WINDOW = 5
ROWS = 384


def kernel(count, heads, named, queries, keys, values, out, *scratch):
    windows = (scratch[:heads], scratch[heads : 2 * heads])
    (held_q, held_o, local_sem, q_sem, o_sem, y_send, y_recv, sib_send, sib_recv,
     z_send, z_recv, share_send, share_recv) = scratch[2 * heads :]
    sources = (keys, values)
    tiles, tile_len, _ = queries.shape
    slots = named.shape[1]
    rows = min(ROWS, tile_len)
    factor = math.log2(math.e) * HD ** -0.5

    me = lax.axis_index("blk")
    core = lax.rem(me, 2)
    side = lax.rem(me // 2, 2)
    quad = me // 4
    last = count // 4 - 1
    sibling = me + 1 - 2 * core
    partner = me + 2 - 4 * side
    ahead = me + 4 - 8 * side
    can_relay = jnp.where(side == 0, quad < last, quad > 0)
    gets_relay = jnp.where(side == 0, quad > 0, quad < last)
    shares_partner = core == side
    partner_at = 4 - 4 * side
    relay_at = 4 * side

    def part(ref, block):
        return ref.at[pl.ds(block * tiles, tiles)]

    def columns(ref, head):
        return ref.at[:, :, pl.ds(head * HD, HD)]

    def local_copy(head, which):
        return pltpu.make_async_copy(
            columns(sources[which], head), part(windows[which][head], 2), local_sem.at[head, which]
        )

    def remote(src, dst, send, recv, head, which, target):
        return pltpu.make_async_remote_copy(
            src_ref=src, dst_ref=dst, send_sem=send.at[head, which], recv_sem=recv.at[head, which],
            device_id={"blk": target}, device_id_type=pl.DeviceIdType.MESH,
        )

    def partner_copy(head, which):
        return remote(columns(sources[which], head), part(windows[which][head], relay_at),
                      y_send, y_recv, head, which, partner)

    def sibling_copy(head, which):
        return remote(columns(sources[which], head), part(windows[which][head], 1 + 2 * core),
                      sib_send, sib_recv, head, which, sibling)

    def relay_copy(head, which):
        window = windows[which][head]
        return remote(part(window, partner_at), part(window, relay_at),
                      z_send, z_recv, head, which, ahead)

    def share_copy(head, which):
        window = windows[which][head]
        return remote(part(window, 4 - 4 * core), part(window, 3 - 2 * core),
                      share_send, share_recv, head, which, sibling)

    def query_copy(head):
        return pltpu.make_async_copy(columns(queries, head), columns(held_q, head), q_sem.at[head])

    def out_copy(head):
        return pltpu.make_async_copy(columns(held_o, head), columns(out, head), o_sem.at[head])

    barrier = pltpu.get_barrier_semaphore()

    def greet(target):
        pl.semaphore_signal(barrier, inc=1, device_id={"blk": target}, device_id_type=pl.DeviceIdType.MESH)

    greet(sibling)
    greet(partner)

    @pl.when(quad > 0)
    def _():
        greet(me - 4)

    @pl.when(quad < last)
    def _():
        greet(me + 4)

    pl.semaphore_wait(barrier, 2 + (quad > 0).astype(jnp.int32) + (quad < last).astype(jnp.int32))

    for head in range(heads):
        for which in range(2):
            partner_copy(head, which).start()
        for which in range(2):
            sibling_copy(head, which).start()
            local_copy(head, which).start()
        query_copy(head).start()

    def attend(head):
        key_window, value_window = windows[0][head], windows[1][head]
        start = head * HD
        per_tile = tile_len // rows

        def block(index, carry):
            tile = index // per_tile
            row = pl.multiple_of(lax.rem(index, per_tile) * rows, rows)
            query = held_q[tile, pl.ds(row, rows), start : start + HD]
            own = 2 * tiles + tile
            base = (me - 2) * tiles
            scores, peaks, valid, places = [], [], [], []
            for slot in range(slots):
                entry = named[tile, slot]
                ok = entry >= 0
                place = jnp.clip(jnp.where(ok, entry - base, own), 0, WINDOW * tiles - 1)
                score = lax.dot_general(
                    query, key_window[place], (((1,), (1,)), ((), ())),
                    preferred_element_type=jnp.float32,
                )
                peak = jnp.max(score, axis=1, keepdims=True)
                peaks.append(jnp.where(ok, peak, -jnp.inf))
                scores.append(score)
                valid.append(ok)
                places.append(place)
            top = functools.reduce(jnp.maximum, peaks) * factor
            total = jnp.zeros((rows, 1), jnp.float32)
            summed = jnp.zeros((rows, HD), jnp.float32)
            for slot in range(slots):
                offset = jnp.where(valid[slot], top, jnp.inf)
                weights = jnp.exp2(scores[slot] * factor - offset)
                total += jnp.sum(weights, axis=1, keepdims=True)
                summed += jnp.dot(
                    weights.astype(jnp.bfloat16), value_window[places[slot]],
                    preferred_element_type=jnp.float32,
                )
            held_o[tile, pl.ds(row, rows), start : start + HD] = (summed / total).astype(held_o.dtype)
            return carry

        lax.fori_loop(0, tiles * per_tile, block, 0)

    for step in range(heads + 1):
        if step < heads:
            for which in range(2):
                partner_copy(step, which).wait_recv()

                @pl.when(can_relay)
                def _():
                    relay_copy(step, which).start()

                @pl.when(shares_partner)
                def _():
                    share_copy(step, which).start()

        if step > 0:
            head = step - 1
            for which in range(2):

                @pl.when(gets_relay)
                def _():
                    relay_copy(head, which).wait_recv()

                    @pl.when(jnp.logical_not(shares_partner))
                    def _():
                        share_copy(head, which).start()

            query_copy(head).wait()
            for which in range(2):
                local_copy(head, which).wait()
                sibling_copy(head, which).wait_recv()

                @pl.when(jnp.logical_or(jnp.logical_not(shares_partner), gets_relay))
                def _():
                    share_copy(head, which).wait_recv()

            attend(head)
            out_copy(head).start()

    for head in range(heads):
        out_copy(head).wait()
        for which in range(2):
            partner_copy(head, which).wait_send()
            sibling_copy(head, which).wait_send()

            @pl.when(can_relay)
            def _():
                relay_copy(head, which).wait_send()

            @pl.when(jnp.logical_or(shares_partner, gets_relay))
            def _():
                share_copy(head, which).wait_send()


def on_device(count, queries, keys, values, neighbours):
    tokens, width = queries.shape
    tiles = neighbours.shape[0]
    tile_len = tokens // tiles
    heads = width // HD
    shape = (tiles, tile_len, width)
    window = pltpu.VMEM((WINDOW * tiles, tile_len, HD), queries.dtype)
    pair = pltpu.SemaphoreType.DMA((heads, 2))
    single = pltpu.SemaphoreType.DMA((heads,))
    hbm = pl.BlockSpec(memory_space=pl.ANY)
    out = pl.pallas_call(
        functools.partial(kernel, count, heads),
        out_shape=jax.ShapeDtypeStruct(shape, queries.dtype),
        in_specs=[pl.BlockSpec(memory_space=pltpu.SMEM), hbm, hbm, hbm],
        out_specs=hbm,
        scratch_shapes=[window] * (2 * heads)
        + [pltpu.VMEM(shape, queries.dtype)] * 2
        + [pair, single, single]
        + [pair] * 8,
        compiler_params=pltpu.CompilerParams(
            collective_id=0, has_side_effects=True, vmem_limit_bytes=60 * 1024 * 1024
        ),
    )(neighbours, queries.reshape(shape), keys.reshape(shape), values.reshape(shape))
    return out.reshape(tokens, width)


def solution(mesh):
    spec = P(("groups", "blk"), None)
    return jax.shard_map(
        functools.partial(on_device, mesh.shape["blk"]),
        mesh=mesh, in_specs=(spec,) * 4, out_specs=spec, check_vma=False,
    )
```

time: 483 us -> 124 us (0.26)
  the two profiles are of different devices: /device:TPU:1 before, /device:TPU:7 now
where the time goes in v1:
time: 124 us
  Pallas kernels  121 us (98%)
  local copies, waits for them, and re-layouts  3.22 us (3%)
    pallas_call x1, Pallas kernels, on_device(): pl.pallas_call(functools.partial(kernel, count, heads), out_shape=jax.Sha...  121 us
    unnamed x1, local copies, waits for them, and re-layouts  3.22 us

profile of v1, /device:TPU:7, one launch (start us, length us, event | category | flops | bytes accessed | tf_op | source)
XLA Modules:
  0.0 123.9 jit_solution(15374692411765399938)
XLA Ops:
  0.0 120.7 %shard_map.46 = bf16[2,384,1536]{2,1,0:T(8,128)(2,1)} custom-call(s32[2,7]{1,0:T(2,128)} %named.1, bf16[2,384,1536]{2,1,0:T(8,128)(2,1)} %bitcast.5, bf16[2,384,1536]{2,1,0:T(8,128)(2,1)} %bitcast.6, bf16[2,384,1536]{2,1,0:T(8,128)(2,1)} %bitcast.7), custom_call_target="tpu_custom_call" | custom-call | tf_op jit(solution)/shard_map/pallas_call | solution.py:210
  120.7 3.2 %copy.6 = bf16[768,1536]{1,0:T(8,128)(2,1)} copy(bf16[768,1536]{1,0:T(8,128)(2,1)} %bitcast.4) | data formatting | bytes 4718592

commit v2 on v1

v2 whole, which is shorter than its diff:
```python
import functools
import math

import jax
import jax.numpy as jnp
from jax import lax
from jax.experimental import pallas as pl
from jax.experimental.pallas import tpu as pltpu
from jax.sharding import PartitionSpec as P

HD = 128
WINDOW = 5
ROWS = 192


def kernel(count, heads, named, queries, keys, values, out, *scratch):
    windows = (scratch[:heads], scratch[heads : 2 * heads])
    (held_q, held_o, held_w, held_t, local_sem, q_sem, o_sem, y_send, y_recv, sib_send, sib_recv,
     z_send, z_recv, share_send, share_recv) = scratch[2 * heads :]
    sources = (keys, values)
    tiles, tile_len, _ = queries.shape
    slots = named.shape[1]
    rows = min(ROWS, tile_len)
    factor = math.log2(math.e) * HD ** -0.5

    me = lax.axis_index("blk")
    core = lax.rem(me, 2)
    side = lax.rem(me // 2, 2)
    quad = me // 4
    last = count // 4 - 1
    sibling = me + 1 - 2 * core
    partner = me + 2 - 4 * side
    ahead = me + 4 - 8 * side
    can_relay = jnp.where(side == 0, quad < last, quad > 0)
    gets_relay = jnp.where(side == 0, quad > 0, quad < last)
    shares_partner = core == side
    partner_at = 4 - 4 * side
    relay_at = 4 * side

    def pieces(head, which):
        return tiles if which == 1 and head >= heads - 2 else 1

    def part(ref, block, piece=0, total=1):
        size = tiles // total
        return ref.at[pl.ds(block * tiles + piece * size, size)]

    def columns(ref, head, piece=0, total=1):
        size = tiles // total
        return ref.at[pl.ds(piece * size, size), :, pl.ds(head * HD, HD)]

    def local_copy(head, which):
        return pltpu.make_async_copy(
            columns(sources[which], head), part(windows[which][head], 2), local_sem.at[head, which]
        )

    def remote(src, dst, send, recv, target):
        return pltpu.make_async_remote_copy(
            src_ref=src, dst_ref=dst, send_sem=send, recv_sem=recv,
            device_id={"blk": target}, device_id_type=pl.DeviceIdType.MESH,
        )

    def partner_copy(head, which, piece):
        at = (head, which, piece)
        cut = (piece, pieces(head, which))
        return remote(columns(sources[which], head, *cut), part(windows[which][head], relay_at, *cut),
                      y_send.at[at], y_recv.at[at], partner)

    def sibling_copy(head, which):
        at = (head, which)
        return remote(columns(sources[which], head), part(windows[which][head], 1 + 2 * core),
                      sib_send.at[at], sib_recv.at[at], sibling)

    def relay_copy(head, which, piece):
        at = (head, which, piece)
        cut = (piece, pieces(head, which))
        window = windows[which][head]
        return remote(part(window, partner_at, *cut), part(window, relay_at, *cut),
                      z_send.at[at], z_recv.at[at], ahead)

    def share_copy(head, which, piece):
        at = (head, which, piece)
        cut = (piece, pieces(head, which))
        window = windows[which][head]
        return remote(part(window, 4 - 4 * core, *cut), part(window, 3 - 2 * core, *cut),
                      share_send.at[at], share_recv.at[at], sibling)

    def query_copy(head):
        return pltpu.make_async_copy(columns(queries, head), columns(held_q, head), q_sem.at[head])

    def out_copy(head):
        return pltpu.make_async_copy(columns(held_o, head), columns(out, head), o_sem.at[head])

    barrier = pltpu.get_barrier_semaphore()

    def greet(target):
        pl.semaphore_signal(barrier, inc=1, device_id={"blk": target}, device_id_type=pl.DeviceIdType.MESH)

    greet(sibling)
    greet(partner)

    @pl.when(quad > 0)
    def _():
        greet(me - 4)

    @pl.when(quad < last)
    def _():
        greet(me + 4)

    pl.semaphore_wait(barrier, 2 + (quad > 0).astype(jnp.int32) + (quad < last).astype(jnp.int32))

    order = [(head, which) for head in range(heads - 2) for which in range(2)]
    order += [(head, which) for which in range(2) for head in range(heads - 2, heads)]
    for head, which in order:
        for piece in range(pieces(head, which)):
            partner_copy(head, which, piece).start()
        sibling_copy(head, which).start()
        local_copy(head, which).start()
        if which == 0:
            query_copy(head).start()

    def over_rows(step):
        def block(index, carry):
            step(pl.ds(pl.multiple_of(index * rows, rows), rows))
            return carry

        lax.fori_loop(0, tile_len // rows, block, 0)

    def entries(tile):
        base = (me - 2) * tiles
        own = 2 * tiles + tile
        found = []
        for slot in range(slots):
            entry = named[tile, slot]
            ok = entry >= 0
            place = jnp.clip(jnp.where(ok, entry - base, own), 0, WINDOW * tiles - 1)
            found.append((ok, place))
        return found

    def weigh(head, tile, at):
        query = held_q[tile, at, head * HD : (head + 1) * HD]
        found = entries(tile)
        scores = [
            lax.dot_general(query, windows[0][head][place], (((1,), (1,)), ((), ())),
                            preferred_element_type=jnp.float32)
            for _, place in found
        ]
        peaks = [
            jnp.where(ok, jnp.max(score, axis=1, keepdims=True), -jnp.inf)
            for score, (ok, _) in zip(scores, found)
        ]
        top = functools.reduce(jnp.maximum, peaks) * factor
        total = jnp.zeros((rows, 1), jnp.float32)
        for slot, (ok, place) in enumerate(found):
            weights = jnp.exp2(scores[slot] * factor - jnp.where(ok, top, jnp.inf))
            total += jnp.sum(weights, axis=1, keepdims=True)
            yield slot, place, weights.astype(jnp.bfloat16)
        yield total

    def attend(head, tile):
        def step(at):
            summed = jnp.zeros((rows, HD), jnp.float32)
            *parts, total = weigh(head, tile, at)
            for _, place, rounded in parts:
                summed += jnp.dot(rounded, windows[1][head][place], preferred_element_type=jnp.float32)
            held_o[tile, at, head * HD : (head + 1) * HD] = (summed / total).astype(held_o.dtype)

        over_rows(step)

    def score(head, tile):
        late = head - (heads - 2)

        def step(at):
            *parts, total = weigh(head, tile, at)
            for slot, _, rounded in parts:
                held_w[late, tile, at, slot * tile_len : (slot + 1) * tile_len] = rounded
            held_t[late, tile, at, :] = jnp.broadcast_to(total, (rows, HD))

        over_rows(step)

    def gather(head, tile):
        late = head - (heads - 2)

        def step(at):
            summed = jnp.zeros((rows, HD), jnp.float32)
            for slot, (_, place) in enumerate(entries(tile)):
                summed += jnp.dot(
                    held_w[late, tile, at, slot * tile_len : (slot + 1) * tile_len],
                    windows[1][head][place], preferred_element_type=jnp.float32,
                )
            result = summed / held_t[late, tile, at, :]
            held_o[tile, at, head * HD : (head + 1) * HD] = result.astype(held_o.dtype)

        over_rows(step)

    def arrive(head, which, piece=0):
        partner_copy(head, which, piece).wait_recv()

        @pl.when(can_relay)
        def _():
            relay_copy(head, which, piece).start()

        @pl.when(shares_partner)
        def _():
            share_copy(head, which, piece).start()

    def finish(head, which):
        for piece in range(pieces(head, which)):

            @pl.when(gets_relay)
            def _():
                relay_copy(head, which, piece).wait_recv()

                @pl.when(jnp.logical_not(shares_partner))
                def _():
                    share_copy(head, which, piece).start()

    def ready(head, which):
        if which == 0:
            query_copy(head).wait()
        local_copy(head, which).wait()
        sibling_copy(head, which).wait_recv()
        for piece in range(pieces(head, which)):

            @pl.when(jnp.logical_or(jnp.logical_not(shares_partner), gets_relay))
            def _():
                share_copy(head, which, piece).wait_recv()

    half = tiles // 2

    def each(work, head, first):
        for tile in range(half) if first else range(half, tiles):
            work(head, tile)

    def both(head):
        for which in range(2):
            finish(head, which)
        for which in range(2):
            ready(head, which)

    for head in range(heads - 2):
        arrive(head, 0)
        if head > 0:
            both(head - 1)
            each(attend, head - 1, True)
        arrive(head, 1)
        if head > 0:
            each(attend, head - 1, False)
            out_copy(head - 1).start()

    early, late = heads - 2, heads - 1
    arrive(early, 0)
    both(early - 1)
    each(attend, early - 1, True)
    arrive(late, 0)
    finish(early, 0)
    each(attend, early - 1, False)
    out_copy(early - 1).start()
    ready(early, 0)
    for piece in range(tiles):
        arrive(early, 1, piece)
        score(early, piece)
    for piece in range(tiles):
        arrive(late, 1, piece)
        if piece == 0:
            finish(late, 0)
            ready(late, 0)
        if piece == tiles - 1:
            finish(early, 1)
        score(late, piece)
    ready(early, 1)
    for tile in range(tiles):
        gather(early, tile)
    out_copy(early).start()
    finish(late, 1)
    ready(late, 1)
    for tile in range(tiles):
        gather(late, tile)
    out_copy(late).start()

    for head in range(heads):
        out_copy(head).wait()
        for which in range(2):
            sibling_copy(head, which).wait_send()
            for piece in range(pieces(head, which)):
                partner_copy(head, which, piece).wait_send()

                @pl.when(can_relay)
                def _():
                    relay_copy(head, which, piece).wait_send()

                @pl.when(jnp.logical_or(shares_partner, gets_relay))
                def _():
                    share_copy(head, which, piece).wait_send()


def on_device(count, queries, keys, values, neighbours):
    tokens, width = queries.shape
    tiles = neighbours.shape[0]
    tile_len = tokens // tiles
    heads = width // HD
    shape = (tiles, tile_len, width)
    window = pltpu.VMEM((WINDOW * tiles, tile_len, HD), queries.dtype)
    slots = neighbours.shape[1]
    pair = pltpu.SemaphoreType.DMA((heads, 2))
    triple = pltpu.SemaphoreType.DMA((heads, 2, tiles))
    single = pltpu.SemaphoreType.DMA((heads,))
    hbm = pl.BlockSpec(memory_space=pl.ANY)
    out = pl.pallas_call(
        functools.partial(kernel, count, heads),
        out_shape=jax.ShapeDtypeStruct(shape, queries.dtype),
        in_specs=[pl.BlockSpec(memory_space=pltpu.SMEM), hbm, hbm, hbm],
        out_specs=hbm,
        scratch_shapes=[window] * (2 * heads)
        + [pltpu.VMEM(shape, queries.dtype)] * 2
        + [pltpu.VMEM((2, tiles, tile_len, slots * tile_len), queries.dtype)]
        + [pltpu.VMEM((2, tiles, tile_len, HD), jnp.float32)]
        + [pair, single, single, triple, triple, pair, pair]
        + [triple] * 4,
        compiler_params=pltpu.CompilerParams(
            collective_id=0, has_side_effects=True, vmem_limit_bytes=60 * 1024 * 1024
        ),
    )(neighbours, queries.reshape(shape), keys.reshape(shape), values.reshape(shape))
    return out.reshape(tokens, width)


def solution(mesh):
    spec = P(("groups", "blk"), None)
    return jax.shard_map(
        functools.partial(on_device, mesh.shape["blk"]),
        mesh=mesh, in_specs=(spec,) * 4, out_specs=spec, check_vma=False,
    )
```

time: 124 us -> 124 us (level)
  no operation moved by 1% of the time
where the time goes in v2:
time: 124 us
  Pallas kernels  121 us (98%)
  local copies, waits for them, and re-layouts  3.22 us (3%)
    pallas_call x1, Pallas kernels, on_device(): pl.pallas_call(functools.partial(kernel, count, heads), out_shape=jax.Sha...  121 us
    unnamed x1, local copies, waits for them, and re-layouts  3.22 us

profile of v2, /device:TPU:7, one launch (start us, length us, event | category | flops | bytes accessed | tf_op | source)
XLA Modules:
  0.0 124.2 jit_solution(10809405506580187807)
XLA Ops:
  0.0 121.0 %shard_map.46 = bf16[2,384,1536]{2,1,0:T(8,128)(2,1)} custom-call(s32[2,7]{1,0:T(2,128)} %named.1, bf16[2,384,1536]{2,1,0:T(8,128)(2,1)} %bitcast.5, bf16[2,384,1536]{2,1,0:T(8,128)(2,1)} %bitcast.6, bf16[2,384,1536]{2,1,0:T(8,128)(2,1)} %bitcast.7), custom_call_target="tpu_custom_call" | custom-call | tf_op jit(solution)/shard_map/pallas_call | solution.py:308
  121.0 3.2 %copy.6 = bf16[768,1536]{1,0:T(8,128)(2,1)} copy(bf16[768,1536]{1,0:T(8,128)(2,1)} %bitcast.4) | data formatting | bytes 4718592

commit v3 on v1

--- a/solution.py
+++ b/solution.py
@@ -104,12 +104,15 @@
             local_copy(head, which).start()
         query_copy(head).start()
 
-    def attend(head):
+    def attend(head, between):
         key_window, value_window = windows[0][head], windows[1][head]
         start = head * HD
         per_tile = tile_len // rows
 
         def block(index, carry):
+            if between is not None:
+                pl.when(index == 1)(between)
+
             tile = index // per_tile
             row = pl.multiple_of(lax.rem(index, per_tile) * rows, rows)
             query = held_q[tile, pl.ds(row, rows), start : start + HD]
@@ -145,18 +148,22 @@
 
         lax.fori_loop(0, tiles * per_tile, block, 0)
 
+    def arrive(head, which):
+        partner_copy(head, which).wait_recv()
+
+        @pl.when(can_relay)
+        def _():
+            relay_copy(head, which).start()
+
+        @pl.when(shares_partner)
+        def _():
+            share_copy(head, which).start()
+
     for step in range(heads + 1):
         if step < heads:
-            for which in range(2):
-                partner_copy(step, which).wait_recv()
-
-                @pl.when(can_relay)
-                def _():
-                    relay_copy(step, which).start()
-
-                @pl.when(shares_partner)
-                def _():
-                    share_copy(step, which).start()
+            arrive(step, 0)
+            if step == 0:
+                arrive(step, 1)
 
         if step > 0:
             head = step - 1
@@ -179,7 +186,7 @@
                 def _():
                     share_copy(head, which).wait_recv()
 
-            attend(head)
+            attend(head, functools.partial(arrive, step, 1) if step < heads else None)
             out_copy(head).start()
 
     for head in range(heads):

time: 124 us -> 124 us (level)
  no operation moved by 1% of the time
where the time goes in v3:
time: 124 us
  Pallas kernels  121 us (98%)
  local copies, waits for them, and re-layouts  3.22 us (3%)
    pallas_call x1, Pallas kernels, on_device(): pl.pallas_call(functools.partial(kernel, count, heads), out_shape=jax.Sha...  121 us
    unnamed x1, local copies, waits for them, and re-layouts  3.22 us

profile of v3, /device:TPU:7, one launch (start us, length us, event | category | flops | bytes accessed | tf_op | source)
XLA Modules:
  0.0 124.3 jit_solution(10693849009828092089)
XLA Ops:
  0.0 121.1 %shard_map.46 = bf16[2,384,1536]{2,1,0:T(8,128)(2,1)} custom-call(s32[2,7]{1,0:T(2,128)} %named.1, bf16[2,384,1536]{2,1,0:T(8,128)(2,1)} %bitcast.5, bf16[2,384,1536]{2,1,0:T(8,128)(2,1)} %bitcast.6, bf16[2,384,1536]{2,1,0:T(8,128)(2,1)} %bitcast.7), custom_call_target="tpu_custom_call" | custom-call | tf_op jit(solution)/shard_map/pallas_call | solution.py:217
  121.1 3.2 %copy.6 = bf16[768,1536]{1,0:T(8,128)(2,1)} copy(bf16[768,1536]{1,0:T(8,128)(2,1)} %bitcast.4) | data formatting | bytes 4718592
